TPU v7x, 256 devices: a whole 4x4x8 slice. The times are simulated.
256 devices in a mesh: head: 8 (over x, z_lo), ctx: 32 (over y, z_hi, core).
Axes of the slice: x: 4, y: 4, z: 8 (z_hi: 4, z_lo: 2; z = z_hi * 2 + z_lo), core: 2. Of those that a mesh axis runs over, the one named last changes fastest.
Arguments:
- queries: bfloat16 [16384, 5120], P(('head', 'ctx')), may hold values from -6 to 6
- keys: bfloat16 [16384, 5120], P(('head', 'ctx')), may hold values from -6 to 6
- values: bfloat16 [16384, 5120], P(('head', 'ctx')), may hold values from -6 to 6
- rates: bfloat16 [16384, 8], P(('head', 'ctx')), may hold values from 0.099609375 to 1
- q_gain: float32 [5120], replicated, may hold values from 0.1 to 1.9
- k_gain: float32 [5120], replicated, may hold values from 0.2 to 4.5, as said below
- w_first: float32 [8, 640, 640], P('head'), may hold values from -0.2766993 to 0.2766993
- w_second: float32 [8, 640, 640], P('head'), may hold values from -0.25 to 0.25
- w_third: float32 [8, 640, 640], P('head'), may hold values from -0.2766993 to 0.2766993
Outputs:
- attended: bfloat16 [16384, 5120], P(('head', 'ctx'))
Inputs may be any that keep to these rules, and one draw needn't show every extreme that they name: `k_gain`: positive per-feature gains.
All inputs are finite; a program needn't handle non-finite values.
Results may differ from a plain program's by a relative error of at most 0.015.
Values may be sent and summed in bfloat16 or wider, within the bound.
A program may use at most 64 MiB of HBM per device.

v0:
```python
import jax
import jax.numpy as jnp
from jax import lax
from jax.sharding import PartitionSpec as P

NS_STEPS = 2


epsilon = 1e-06
frob_eps = 1e-07
coeff_a = 3.4445
coeff_b = -4.775
coeff_c = 2.0315
step_size = 1.0


def rms_scale(inputs, gain):
    widened = inputs.astype(jnp.float32)
    factor = lax.rsqrt(jnp.mean(widened * widened, axis=-1, keepdims=True) + epsilon)
    return (widened * factor * gain).astype(jnp.bfloat16)


def update_rows(own_rows, square_rows, full_square, full_iterate):
    polynomial = (
        coeff_b * square_rows.astype(jnp.float32)
        + coeff_c
        * jnp.einsum("hij,hjk->hik", square_rows, full_square, preferred_element_type=jnp.float32)
    ).astype(jnp.bfloat16)
    return (
        coeff_a * own_rows.astype(jnp.float32)
        + jnp.einsum("hij,hjk->hik", polynomial, full_iterate, preferred_element_type=jnp.float32)
    ).astype(jnp.bfloat16)


def orthogonal(gradient):
    frob_total = jnp.sqrt(jnp.sum(gradient * gradient, axis=(1, 2), keepdims=True))
    iterate = (gradient / (frob_total + frob_eps)).astype(jnp.bfloat16)
    for repeat_index in range(NS_STEPS):
        square = jnp.einsum(
            "hij,hkj->hik", iterate, iterate, preferred_element_type=jnp.float32
        ).astype(jnp.bfloat16)
        iterate = update_rows(iterate, square, square, iterate)
    return iterate


def per_device(queries, keys, values, rates, q_gain, k_gain, w_first, w_second, w_third):
    queries_n = rms_scale(queries, q_gain)
    keys_n = rms_scale(keys, k_gain)
    arrived = (
        lax.all_to_all(queries_n, "head", split_axis=1, concat_axis=0, tiled=True),
        lax.all_to_all(keys_n, "head", split_axis=1, concat_axis=0, tiled=True),
        lax.all_to_all(values, "head", split_axis=1, concat_axis=0, tiled=True),
        lax.all_to_all(rates, "head", split_axis=1, concat_axis=0, tiled=True),
    )
    heads_here = w_first.shape[0]
    width = w_first.shape[1]
    token_rows = arrived[0].shape[0]
    query_local = arrived[0].reshape(token_rows, heads_here, width)
    key_local = arrived[1].reshape(token_rows, heads_here, width)
    value_local = arrived[2].reshape(token_rows, heads_here, width)
    rate_local = arrived[3]
    first_b = w_first.astype(jnp.bfloat16)
    second_b = w_second.astype(jnp.bfloat16)
    third_b = w_third.astype(jnp.bfloat16)
    pre_first = jnp.einsum("thd,hde->the", key_local, first_b, preferred_element_type=jnp.float32)
    pre_third = jnp.einsum("thd,hde->the", key_local, third_b, preferred_element_type=jnp.float32)
    sigmoid = jax.nn.sigmoid(pre_first)
    activ = pre_first * sigmoid
    hidden = (activ * pre_third).astype(jnp.bfloat16)
    scaled_v = (
        rate_local[:, :, None].astype(jnp.float32) * value_local.astype(jnp.float32)
    ).astype(jnp.bfloat16)
    back_hidden = jnp.einsum("the,hde->thd", scaled_v, second_b, preferred_element_type=jnp.float32)
    grad_pre_first = (
        back_hidden * pre_third * sigmoid * (1.0 + pre_first * (1.0 - sigmoid))
    ).astype(jnp.bfloat16)
    grad_pre_third = (back_hidden * activ).astype(jnp.bfloat16)
    grad_first = jnp.einsum(
        "thd,the->hde", key_local, grad_pre_first, preferred_element_type=jnp.float32
    )
    grad_second = jnp.einsum("thd,the->hde", hidden, scaled_v, preferred_element_type=jnp.float32)
    grad_third = jnp.einsum(
        "thd,the->hde", key_local, grad_pre_third, preferred_element_type=jnp.float32
    )
    full_first, full_second, full_third = lax.psum((grad_first, grad_second, grad_third), "ctx")
    new_first = (w_first + step_size * orthogonal(full_first).astype(jnp.float32)).astype(
        jnp.bfloat16
    )
    new_second = (w_second + step_size * orthogonal(full_second).astype(jnp.float32)).astype(
        jnp.bfloat16
    )
    new_third = (w_third + step_size * orthogonal(full_third).astype(jnp.float32)).astype(
        jnp.bfloat16
    )
    query_first = jnp.einsum(
        "thd,hde->the", query_local, new_first, preferred_element_type=jnp.float32
    )
    query_third = jnp.einsum(
        "thd,hde->the", query_local, new_third, preferred_element_type=jnp.float32
    )
    gated = (jax.nn.silu(query_first) * query_third).astype(jnp.bfloat16)
    result = jnp.einsum("thd,hde->the", gated, new_second, preferred_element_type=jnp.float32)
    normed = (
        result * lax.rsqrt(jnp.mean(result * result, axis=-1, keepdims=True) + epsilon)
    ).astype(jnp.bfloat16)
    return lax.all_to_all(
        normed.reshape(token_rows, heads_here * width),
        "head",
        split_axis=0,
        concat_axis=1,
        tiled=True,
    )


def solution(mesh):
    return jax.shard_map(
        per_device,
        mesh=mesh,
        in_specs=(
            P(("head", "ctx"), None),
            P(("head", "ctx"), None),
            P(("head", "ctx"), None),
            P(("head", "ctx"), None),
            P(),
            P(),
            P("head", None, None),
            P("head", None, None),
            P("head", None, None),
        ),
        out_specs=P(("head", "ctx"), None),
        check_vma=False,
    )
```

profile of v0, /device:TPU:1, one launch (start us, length us, event | category | flops | bytes accessed | tf_op | source)
XLA Modules:
  0.0 444.8 jit_solution(1477127422497959783)
XLA Ops:
  6.5 1.3 copy.29
  7.8 6.2 %all-to-all-start.1 = ((bf16[64,8,1]{0,2,1:T(2,128)(2,1)}), bf16[64,8,1]{0,2,1:T(2,128)(2,1)S(1)}, u32[]{:S(2)}, u32[]{:S(2)}) async-start(bf16[64,8,1]{0,2,1:T(2,128)(2,1)} %copy.29), calls=%async_computation.1 | async-start | bytes 8192 | tf_op jit(solution)/shard_map/all_to_all | solution.py:53
  14.0 1.3 fusion.8
  15.3 1.3 fusion.10
  16.7 0.0 copy-start.8
  16.7 0.9 copy.45
  17.6 1.4 all-to-all-done.1
  19.0 3.7 all-to-all-start
  22.7 0.0 copy-start.1
  22.7 0.0 copy-done.8
  22.7 0.9 copy.44
  23.7 8.7 %all-to-all-done = bf16[64,8,640]{2,0,1:T(8,128)(2,1)S(1)} async-done(((bf16[64,8,640]{2,0,1:T(8,128)(2,1)}), bf16[64,8,640]{2,0,1:T(8,128)(2,1)S(1)}, u32[]{:S(2)}, u32[]{:S(2)}) %all-to-all-start) | async-done | bytes 655392 | tf_op jit(solution)/shard_map/all_to_all | solution.py:51
  32.4 3.5 all-to-all-start.2
  35.9 0.0 all-reduce.3.cloned.1.call-start
  36.0 0.1 reshape.348
  36.1 0.0 copy-done.1
  36.1 0.0 copy-start.2
  36.1 1.8 convolution_bitcast_fusion.8
  37.9 0.0 copy-done.2
  37.9 1.8 convolution_bitcast_fusion.7
  39.7 4.6 %all-to-all-done.2 = bf16[64,8,640]{2,0,1:T(8,128)(2,1)S(1)} async-done(((bf16[64,8,640]{2,0,1:T(8,128)(2,1)}), bf16[64,8,640]{2,0,1:T(8,128)(2,1)S(1)}, u32[]{:S(2)}, u32[]{:S(2)}) %all-to-all-start.2) | async-done | bytes 655392 | tf_op jit(solution)/shard_map/all_to_all | solution.py:52
  44.3 0.0 copy-start.5
  44.3 0.1 convert_element_type.307
  44.4 1.3 copy-done.5
  45.7 0.8 convolution_bitcast_fusion.6
  46.5 0.5 copy-done.6
  47.0 2.0 convolution_bitcast_fusion
  49.0 0.0 copy-done.7
  49.0 2.1 convolution_bitcast_fusion.1
  51.1 2.1 convolution_bitcast_fusion.2
  53.2 0.0 all-reduce.3.cloned.1.call-update
  53.3 1.1 copy-done
  54.3 0.2 fusion.11
  54.6 0.0 copy-done.9
  54.6 0.2 fusion.13
  54.8 0.9 copy.46
  55.7 3.7 all-to-all-start.3
  59.4 305.2 %all-reduce.3.cloned.1.call-done = (f32[1,640,640]{2,1,0:T(8,128)}, f32[1,640,640]{2,1,0:T(8,128)}, f32[1,640,640]{2,1,0:T(8,128)}) async-done(((f32[1,640,640]{2,1,0:T(8,128)}, f32[1,640,640]{2,1,0:T(8,128)}, f32[1,640,640]{2,1,0:T(8,128)}), (f32[1,640,640]{2,1,0:T(8,128)}, f32[1,640,640]{2,1,0:T(8,128)}, f32[1,640,640]{2,1,0:T(8,128)})) %all-reduce.3.cloned.1.call-update) | async-done | bytes 4915216 | tf_op jit(solution)/shard_map/psum | solution.py:85
  364.6 2.5 multiply_reduce_fusion.2
  367.8 3.8 convolution_convert_fusion.5
  371.6 4.5 %fusion.5 = bf16[1,640,640]{2,1,0:T(8,128)(2,1)S(1)} fusion(bf16[640,640]{1,0:T(8,128)(2,1)} %convolution_convert_fusion.5, f32[1,640,640]{2,1,0:T(8,128)} %get-tuple-element.7, f32[]{:T(128)S(6)} %add.108), kind=kOutput, calls=%fused_computation.11 | convolution fusion | flops 1053900800 | bytes 3276804 | tf_op jit(solution)/shard_map/hij,hjk->hik/dot_general | solution.py:31
  376.1 0.0 copy-start.10
  376.1 0.0 copy-start.4
  376.1 1.8 convolution_convert_fusion.4
  377.9 0.0 copy-done.4
  377.9 2.5 multiply_reduce_fusion
  380.4 0.0 copy-done.10
  381.0 2.8 convolution_convert_fusion.1
  383.8 4.5 %fusion.1 = bf16[1,640,640]{2,1,0:T(8,128)(2,1)} fusion(bf16[640,640]{1,0:T(8,128)(2,1)S(1)} %convolution_convert_fusion.1, f32[1,640,640]{2,1,0:T(8,128)} %get-tuple-element.6, f32[]{:T(128)S(6)} %add.123), kind=kOutput, calls=%fused_computation.3 | convolution fusion | flops 1053900800 | bytes 3276804 | tf_op jit(solution)/shard_map/hij,hjk->hik/dot_general | solution.py:31
  388.3 2.3 convolution_convert_fusion
  391.2 3.8 convolution_convert_fusion.3
  395.0 5.2 %fusion.3 = bf16[1,640,640]{2,1,0:T(8,128)(2,1)} fusion(bf16[640,640]{1,0:T(8,128)(2,1)} %convolution_convert_fusion.3, f32[1,640,640]{2,1,0:T(8,128)} %get-tuple-element.5, f32[]{:T(128)S(6)} %add.115), kind=kOutput, calls=%fused_computation.7 | convolution fusion | flops 1053900800 | bytes 3276804 | tf_op jit(solution)/shard_map/hij,hjk->hik/dot_general | solution.py:31
  400.2 3.2 convolution_convert_fusion.2
  403.4 1.8 add_convert_fusion.1
  405.2 4.4 fusion.15
  409.6 5.1 %fusion.16 = bf16[640,640]{1,0:T(8,128)(2,1)} fusion(f32[1,640,640]{2,1,0:T(8,128)S(1)} %copy-done.1, bf16[1,640,640]{2,1,0:T(8,128)(2,1)} %fusion.3, bf16[640,640]{1,0:T(8,128)(2,1)} %convolution_convert_fusion.2), kind=kOutput, calls=%fused_computation.63 | convolution fusion | flops 1053491200 | bytes 4096000 | tf_op jit(solution)/shard_map/hij,hjk->hik/dot_general | solution.py:31
  414.7 0.0 all-to-all-done.3
  414.7 3.1 convolution_bitcast_fusion.5
  417.7 0.0 copy-done.3
  417.7 4.4 fusion.18
  422.1 1.9 multiply_reduce_fusion.3
  424.1 0.2 multiply_convert_fusion
  424.2 12.8 %all_to_all.77 = bf16[8,64,640]{2,1,0:T(8,128)(2,1)S(1)} all-to-all(bf16[8,64,640]{2,1,0:T(8,128)(2,1)S(1)} %bitcast.199), channel_id=1, replica_groups=mesh['head'=8,'ctx'=32] {'head'}, dimensions={0} | all-to-all | bytes 1310720 | tf_op jit(solution)/shard_map/all_to_all | solution.py:106
  437.0 0.9 copy.40
  (9 shorter events, 0.0 us)
Async XLA Ops:
  7.8 11.2 %all-to-all-start.1 = ((bf16[64,8,1]{0,2,1:T(2,128)(2,1)}), bf16[64,8,1]{0,2,1:T(2,128)(2,1)S(1)}, u32[]{:S(2)}, u32[]{:S(2)}) async-start(bf16[64,8,1]{0,2,1:T(2,128)(2,1)} %copy.29), calls=%async_computation.1 | async-start | bytes 8192 | tf_op jit(solution)/shard_map/all_to_all | solution.py:53
  16.7 6.1 %copy-start.8 = (bf16[64,5120]{1,0:T(8,128)(2,1)S(1)}, bf16[64,5120]{1,0:T(8,128)(2,1)}, u32[]{:S(2)}) copy-start(bf16[64,5120]{1,0:T(8,128)(2,1)} %param.11) | copy-start | bytes 1966084
  19.0 13.3 %all-to-all-start = ((bf16[64,8,640]{2,0,1:T(8,128)(2,1)}), bf16[64,8,640]{2,0,1:T(8,128)(2,1)S(1)}, u32[]{:S(2)}, u32[]{:S(2)}) async-start(bf16[64,8,640]{2,0,1:T(8,128)(2,1)} %bitcast.191), calls=%async_computation | async-start | bytes 1310720 | tf_op jit(solution)/shard_map/all_to_all | solution.py:51
  22.7 13.3 %copy-start.1 = (f32[1,640,640]{2,1,0:T(8,128)S(1)}, f32[1,640,640]{2,1,0:T(8,128)}, u32[]{:S(2)}) copy-start(f32[1,640,640]{2,1,0:T(8,128)} %param.15) | copy-start | bytes 4915204
  32.4 11.9 %all-to-all-start.2 = ((bf16[64,8,640]{2,0,1:T(8,128)(2,1)}), bf16[64,8,640]{2,0,1:T(8,128)(2,1)S(1)}, u32[]{:S(2)}, u32[]{:S(2)}) async-start(bf16[64,8,640]{2,0,1:T(8,128)(2,1)} %bitcast.190), calls=%async_computation.2 | async-start | bytes 1310720 | tf_op jit(solution)/shard_map/all_to_all | solution.py:52
  35.9 328.7 %all-reduce.3.cloned.1.call-start = ((), (), s32[]{:S(2)}) async-start(), calls=%async_computation.5 | async-start | bytes 9830400 | tf_op jit(solution)/shard_map/psum | solution.py:85
  36.1 1.8 copy-start.2
  44.3 1.4 copy-start.5
  45.7 1.3 copy-start.6
  47.0 2.0 copy-start.7
  53.2 1.1 copy-start
  53.2 1.3 copy-start.9
  55.7 359.0 %all-to-all-start.3 = ((bf16[64,8,640]{2,0,1:T(8,128)(2,1)}), bf16[64,8,640]{2,0,1:T(8,128)(2,1)S(1)}, u32[]{:S(2)}, u32[]{:S(2)}) async-start(bf16[64,8,640]{2,0,1:T(8,128)(2,1)} %bitcast.192), calls=%async_computation.3 | async-start | bytes 1310720 | tf_op jit(solution)/shard_map/all_to_all | solution.py:50
  376.1 4.3 copy-start.10
  376.1 1.8 copy-start.4
  414.7 3.1 copy-start.3
Sparse Core Ops, SparseCore 0:
  53.4 311.1 all-reduce.2
where the time goes:
time: 446 us; the launch traced here: 445 us
  waiting for transfers between devices  320 us (72%)
  matrix products  63.2 us (14%)
  starting transfers between devices  17.2 us (4%)
  between operations  15.5 us (3%)
  blocking collectives  12.8 us (3%)
  other arithmetic  8.36 us (2%)
  local copies, waits for them, and re-layouts  7.9 us (2%)
    psum x1, waiting for transfers between devices, per_device(): lax.psum((grad_first, grad_second, grad_third), 'ctx')  305 us
    dot_general x5, matrix products, update_rows(): jnp.einsum('hij,hjk->hik', polynomial, full_iterate, preferred_element_ty...  23.6 us
    dot_general x6, matrix products, orthogonal(): jnp.einsum('hij,hkj->hik', iterate, iterate, preferred_element_type=jnp.f...  17.7 us
    all_to_all x1, blocking collectives, per_device(): lax.all_to_all(normed.reshape(token_rows, heads_here * width), 'head', sp...  12.8 us
  transfers between devices with their start and end apart: 5, of which 4 were waited for; matrix products, arithmetic and copies ran while one was open for 13% of the time, Pallas kernels for 0%

commit v1 on v0

v1 whole, which is shorter than its diff:
```python
import functools

import jax
import jax.numpy as jnp
from jax import lax
from jax.experimental import pallas as pl
from jax.experimental.pallas import tpu as pltpu
from jax.sharding import PartitionSpec as P

MESH = pl.DeviceIdType.MESH
F32 = jnp.float32
BF16 = jnp.bfloat16

epsilon = 1e-06
frob_eps = 1e-07
coeff_a = 3.4445
coeff_b = -4.775
coeff_c = 2.0315
step_size = 1.0

NY, NZ = 4, 4
PIECE = 24


def dot(a, b):
    return jnp.dot(a, b, preferred_element_type=F32)


def dot_t(a, b):
    return lax.dot_general(a, b, (((1,), (1,)), ((), ())), preferred_element_type=F32)


def kernel(
    nh,
    q_ref, k_ref, v_ref, r_ref, qg_ref, kg_ref, w1_hbm, w2_hbm, w3_hbm,
    out_ref,
    sent, got, wf, wb, t1, t3, hid, d1, d3, kt, ht,
    own, cs, cr, ys, yr, zq, zs, zr, zg, x0, xs, xm, x1, u, fw, ob, orx,
    w_sem, a_ss, a_rs, c_ss, c_rs, y_ss, y_rs, z_ss, z_rs, zg_ss, zg_rs,
    yg_ss, yg_rs, cg_ss, cg_rs, o_ss, o_rs,
):
    me_h = lax.axis_index("head")
    me_c = lax.axis_index("ctx")
    y = me_c // (2 * NZ)
    z = (me_c // 2) % NZ
    core = me_c % 2
    tok, width = sent.shape[2], sent.shape[3]
    half = width // 2
    block = half // NY

    def head_peer(s):
        return (me_h + s) % nh

    def ctx_of(yy, zz, cc):
        return (yy * NZ + zz) * 2 + cc

    def y_dev(yy):
        return (me_h, ctx_of(yy, z, core))

    def z_dev(zz):
        return (me_h, ctx_of(y, zz, core))

    core_dev = (me_h, ctx_of(y, z, 1 - core))

    def remote(src, dst, ss, rs, dev):
        return pltpu.make_async_remote_copy(
            src_ref=src, dst_ref=dst, send_sem=ss, recv_sem=rs, device_id=dev, device_id_type=MESH
        )

    w_copies = [
        pltpu.make_async_copy(w.at[0], wf.at[i], w_sem.at[i])
        for i, w in enumerate((w1_hbm, w2_hbm, w3_hbm))
    ]
    for copy in w_copies:
        copy.start()

    barrier = pltpu.get_barrier_semaphore()

    def greet(dev):
        pl.semaphore_signal(barrier, inc=1, device_id=dev, device_id_type=MESH)

    for s in range(1, nh):
        greet((head_peer(s), me_c))
    for s in range(1, NY):
        greet(y_dev((y + s) % NY))
    for s in range(1, NZ):
        greet(z_dev((z + s) % NZ))
    greet(core_dev)

    def normalize(x_ref, g_ref, t):
        total = jnp.zeros((tok, 1), F32)
        for j in range(nh):
            x = x_ref[:, j * width : (j + 1) * width].astype(F32)
            total = total + jnp.sum(x * x, axis=-1, keepdims=True)
        factor = lax.rsqrt(total / (nh * width) + epsilon)
        for j in range(nh):
            cols = slice(j * width, (j + 1) * width)
            sent[t, j] = (x_ref[:, cols].astype(F32) * factor * g_ref[:, cols]).astype(BF16)

    def exchange(t):
        def step(s, carry):
            j = head_peer(s)
            remote(
                sent.at[t, j], got.at[t, me_h], a_ss.at[t, j], a_rs.at[t, me_h], (j, me_c)
            ).start()
            return carry

        lax.fori_loop(1, nh, step, 0)
        got[t, me_h] = sent[t, me_h]

    def arrived(t):
        def step(s, carry):
            j = head_peer(s)
            remote(
                sent.at[t, j], got.at[t, j], a_ss.at[t, j], a_rs.at[t, j], (j, me_c)
            ).wait()
            return carry

        lax.fori_loop(1, nh, step, 0)

    normalize(k_ref, kg_ref, 0)
    pl.semaphore_wait(barrier, nh - 1 + NY - 1 + NZ - 1 + 1)
    exchange(0)
    rate = r_ref[...].astype(F32)
    for j in range(nh):
        cols = slice(j * width, (j + 1) * width)
        sent[1, j] = (rate[:, j : j + 1] * v_ref[:, cols].astype(F32)).astype(BF16)
    exchange(1)
    normalize(q_ref, qg_ref, 2)
    exchange(2)

    for i in range(3):
        w_copies[i].wait()
        wb[i] = wf[i].astype(BF16)

    tokens = nh * tok
    chunk = 2 * tok
    n_chunks = tokens // chunk

    def rows_of(t, i):
        return got[t, pl.ds(2 * i, 2)].reshape(chunk, width)

    arrived(0)

    def first(i, carry):
        rows = pl.ds(pl.multiple_of(i * chunk, chunk), chunk)
        keys = rows_of(0, i)
        p1 = dot(keys, wb[0])
        p3 = dot(keys, wb[2])
        sig = jax.nn.sigmoid(p1)
        act = p1 * sig
        hid[rows] = (act * p3).astype(BF16)
        t3[rows] = act
        t1[rows] = p3 * sig * (1.0 + p1 * (1.0 - sig))
        return carry

    lax.fori_loop(0, n_chunks, first, 0)
    for i in range(n_chunks):
        kt[:, i * chunk : (i + 1) * chunk] = rows_of(0, i).T
        ht[:, i * chunk : (i + 1) * chunk] = hid[i * chunk : (i + 1) * chunk].T
    arrived(1)

    def second(i, carry):
        rows = pl.ds(pl.multiple_of(i * chunk, chunk), chunk)
        back = dot_t(rows_of(1, i), wb[1])
        d1[rows] = (back * t1[rows]).astype(BF16)
        d3[rows] = (back * t3[rows]).astype(BF16)
        return carry

    lax.fori_loop(0, n_chunks, second, 0)

    def half_rows(cc):
        return pl.ds(pl.multiple_of(cc * half, half), half)

    def core_copy(m):
        return remote(cs.at[m], cr.at[m], c_ss.at[m], c_rs.at[m], core_dev)

    def gradient(m, left, right):
        cs[m] = dot(left[half_rows(1 - core)], right).astype(BF16)
        core_copy(m).start()
        own[m] = dot(left[half_rows(core)], right)

    def y_rows(j):
        return pl.ds(pl.multiple_of(j * block, block), block)

    def z_rows(j):
        return pl.ds(pl.multiple_of(j * 16 + (j // 2) * 8, 8), PIECE)

    def y_copy(m, j, src):
        return remote(ys.at[m, j], yr.at[m, src], y_ss.at[m, j], y_rs.at[m, src], y_dev(j))

    def z_copy(m, j, src):
        return remote(zs.at[m, j], zr.at[m, src], z_ss.at[m, j], z_rs.at[m, src], z_dev(j))

    def zg_copy(m, j, src):
        return remote(zg.at[m, src], zg.at[m, src], zg_ss.at[m, j], zg_rs.at[m, src], z_dev(j))

    def yg_copy(m, j, src):
        slot = x0.at[m, core, src]
        return remote(slot, slot, yg_ss.at[m, j], yg_rs.at[m, src], y_dev(j))

    def cg_copy(m, cc):
        slot = x0.at[m, cc]
        return remote(slot, slot, cg_ss.at[m], cg_rs.at[m], core_dev)

    def start_y(m):
        core_copy(m).wait()
        own[m] = own[m] + cr[m].astype(F32)
        for s in range(1, NY):
            j = (y + s) % NY
            ys[m, j] = own[m, y_rows(j)].astype(BF16)
            y_copy(m, j, y).start()

    def start_z(m):
        total = own[m, y_rows(y)]
        for s in range(1, NY):
            j = (y + s) % NY
            y_copy(m, j, y).wait_send()
            y_copy(m, j, j).wait_recv()
            total = total + yr[m, j].astype(F32)
        zq[m] = total
        for s in range(1, NZ):
            j = (z + s) % NZ
            zs[m, j] = zq[m, z_rows(j)].astype(BF16)
            z_copy(m, j, z).start()

    def start_zg(m):
        total = zq[m, z_rows(z)]
        for s in range(1, NZ):
            j = (z + s) % NZ
            z_copy(m, j, z).wait_send()
            z_copy(m, j, j).wait_recv()
            total = total + zr[m, j].astype(F32)
        zg[m, z] = total.astype(BF16)
        for s in range(1, NZ):
            zg_copy(m, (z + s) % NZ, z).start()

    def start_yg(m):
        for s in range(1, NZ):
            j = (z + s) % NZ
            zg_copy(m, j, z).wait_send()
            zg_copy(m, j, j).wait_recv()
        parts = [zg[m, j].astype(F32) for j in range(NZ)]
        whole = jnp.concatenate([parts[0][:16], parts[1], parts[2][:16], parts[3]], axis=0)
        x0[m, core, y] = whole.astype(BF16)
        for s in range(1, NY):
            yg_copy(m, (y + s) % NY, y).start()

    def start_cg(m):
        for s in range(1, NY):
            j = (y + s) % NY
            yg_copy(m, j, y).wait_send()
            yg_copy(m, j, j).wait_recv()
        cg_copy(m, core).start()

    def halves(fn):
        def step(i, carry):
            fn(i, pl.ds(pl.multiple_of(i * half, half), half))
            return carry

        lax.fori_loop(0, 2, step, 0)

    def ns_steps(m, w_index):
        cell = {}

        def grad_half(i):
            return x0[m, i].reshape(half, width)

        def grad_full():
            return x0[m].reshape(width, width)

        def square0():
            cg_copy(m, core).wait_send()
            cg_copy(m, 1 - core).wait_recv()
            total = jnp.zeros((1, 1), F32)
            for i in range(2):
                g = grad_half(i).astype(F32)
                total = total + jnp.sum(g * g, axis=(0, 1), keepdims=True)
            inv = 1.0 / (jnp.sqrt(total) + frob_eps)
            cell["inv"] = inv

            def fn(i, rows):
                xs[rows] = (dot_t(grad_half(i), grad_full()) * inv * inv).astype(BF16)

            halves(fn)

        def poly():
            def fn(i, rows):
                s = xs[rows]
                xm[rows] = (coeff_b * s.astype(F32) + coeff_c * dot(s, xs[...])).astype(BF16)

            halves(fn)

        def step0():
            inv = cell["inv"]

            def fn(i, rows):
                g = grad_half(i).astype(F32)
                x1[rows] = ((coeff_a * g + dot(xm[rows], grad_full())) * inv).astype(BF16)

            halves(fn)

        def square1():
            def fn(i, rows):
                xs[rows] = dot_t(x1[rows], x1[...]).astype(BF16)

            halves(fn)

        def step1():
            def fn(i, rows):
                new = (coeff_a * x1[rows].astype(F32) + dot(xm[rows], x1[...])).astype(BF16)
                u[m, rows] = (wf[w_index, rows] + step_size * new.astype(F32)).astype(BF16)

            halves(fn)

        return [square0, poly, step0, square1, poly, step1]

    gradient(0, kt, d3[...])
    gradient(1, kt, d1[...])
    start_y(0)
    gradient(2, ht, got[1].reshape(tokens, width))
    start_y(1)
    start_y(2)
    start_z(0)
    start_z(1)
    start_zg(0)
    start_z(2)
    start_zg(1)
    start_yg(0)
    start_zg(2)
    start_yg(1)
    start_cg(0)
    ns0 = ns_steps(0, 2)
    ns0[0]()
    start_yg(2)
    ns0[1]()
    ns0[2]()
    start_cg(1)
    ns0[3]()
    ns0[4]()
    start_cg(2)
    ns0[5]()
    for fn in ns_steps(1, 0):
        fn()

    arrived(2)

    def gate(i, carry):
        rows = pl.ds(pl.multiple_of(i * chunk, chunk), chunk)
        queries = rows_of(2, i)
        a = dot(queries, u[1])
        b = dot(queries, u[0])
        fw[rows] = (a * jax.nn.sigmoid(a) * b).astype(BF16)
        return carry

    lax.fori_loop(0, n_chunks, gate, 0)
    for fn in ns_steps(2, 1):
        fn()

    def o_copy(j, src):
        return remote(ob.at[j], orx.at[src], o_ss.at[j], o_rs.at[src], (j, me_c))

    mine = me_h // 2

    def finish(i):
        c = (mine + i) % n_chunks
        rows = pl.ds(pl.multiple_of(c * chunk, chunk), chunk)
        o = dot(fw[rows], u[2])
        o = o * lax.rsqrt(jnp.mean(o * o, axis=-1, keepdims=True) + epsilon)
        ob[pl.ds(2 * c, 2)] = o.astype(BF16).reshape(2, tok, width)
        return c

    def others(i, carry):
        c = finish(i)
        o_copy(2 * c, me_h).start()
        o_copy(2 * c + 1, me_h).start()
        return carry

    lax.fori_loop(1, n_chunks, others, 0)
    finish(0)
    twin = mine * 2 + (1 - me_h % 2)
    o_copy(twin, me_h).start()
    orx[me_h] = ob[me_h]

    def back(s, carry):
        j = head_peer(s)
        o_copy(j, me_h).wait_send()
        o_copy(j, j).wait_recv()
        return carry

    lax.fori_loop(1, nh, back, 0)
    for j in range(nh):
        out_ref[:, j * width : (j + 1) * width] = orx[j]


def per_device(queries, keys, values, rates, q_gain, k_gain, w_first, w_second, w_third):
    nh = rates.shape[1]
    tok, model = queries.shape
    width = model // nh
    tokens = nh * tok
    half, block = width // 2, width // 2 // NY
    vmem = pl.BlockSpec(memory_space=pltpu.VMEM)
    hbm = pl.BlockSpec(memory_space=pl.ANY)
    dma = pltpu.SemaphoreType.DMA
    return pl.pallas_call(
        functools.partial(kernel, nh),
        out_shape=jax.ShapeDtypeStruct((tok, model), BF16),
        in_specs=[vmem] * 6 + [hbm] * 3,
        out_specs=vmem,
        scratch_shapes=[
            pltpu.VMEM((3, nh, tok, width), BF16),
            pltpu.VMEM((3, nh, tok, width), BF16),
            pltpu.VMEM((3, width, width), F32),
            pltpu.VMEM((3, width, width), BF16),
            pltpu.VMEM((tokens, width), F32),
            pltpu.VMEM((tokens, width), F32),
            pltpu.VMEM((tokens, width), BF16),
            pltpu.VMEM((tokens, width), BF16),
            pltpu.VMEM((tokens, width), BF16),
            pltpu.VMEM((width, tokens), BF16),
            pltpu.VMEM((width, tokens), BF16),
            pltpu.VMEM((3, half, width), F32),
            pltpu.VMEM((3, half, width), BF16),
            pltpu.VMEM((3, half, width), BF16),
            pltpu.VMEM((3, NY, block, width), BF16),
            pltpu.VMEM((3, NY, block, width), BF16),
            pltpu.VMEM((3, block, width), F32),
            pltpu.VMEM((3, NZ, PIECE, width), BF16),
            pltpu.VMEM((3, NZ, PIECE, width), BF16),
            pltpu.VMEM((3, NZ, PIECE, width), BF16),
            pltpu.VMEM((3, 2, NY, block, width), BF16),
            pltpu.VMEM((width, width), BF16),
            pltpu.VMEM((width, width), BF16),
            pltpu.VMEM((width, width), BF16),
            pltpu.VMEM((3, width, width), BF16),
            pltpu.VMEM((tokens, width), BF16),
            pltpu.VMEM((nh, tok, width), BF16),
            pltpu.VMEM((nh, tok, width), BF16),
            dma((3,)),
            dma((3, nh)), dma((3, nh)),
            dma((3,)), dma((3,)),
            dma((3, NY)), dma((3, NY)),
            dma((3, NZ)), dma((3, NZ)),
            dma((3, NZ)), dma((3, NZ)),
            dma((3, NY)), dma((3, NY)),
            dma((3,)), dma((3,)),
            dma((nh,)), dma((nh,)),
        ],
        compiler_params=pltpu.CompilerParams(
            collective_id=0, has_side_effects=True, vmem_limit_bytes=58 * 2**20
        ),
        name="span",
    )(
        queries, keys, values, rates, q_gain.reshape(1, model), k_gain.reshape(1, model),
        w_first, w_second, w_third,
    )


def solution(mesh):
    return jax.shard_map(
        per_device,
        mesh=mesh,
        in_specs=(
            P(("head", "ctx"), None),
            P(("head", "ctx"), None),
            P(("head", "ctx"), None),
            P(("head", "ctx"), None),
            P(),
            P(),
            P("head", None, None),
            P("head", None, None),
            P("head", None, None),
        ),
        out_specs=P(("head", "ctx"), None),
        check_vma=False,
    )
```

time: 446 us -> 102 us (0.23)
  waiting for transfers between devices: 320 us -> 0 us
  Pallas kernels: 0 us -> 98.4 us
  matrix products: 63.2 us -> 0 us
  starting transfers between devices: 17.2 us -> 0 us
  between operations: 15.5 us -> 0.01 us
  blocking collectives: 12.8 us -> 0 us
  other arithmetic: 8.36 us -> 0 us
  local copies, waits for them, and re-layouts: 7.9 us -> 3.34 us
    psum x1 -> x0, waiting for transfers between devices: 305 us -> none  [per_device(): lax.psum((grad_first, grad_second, grad_third), 'ctx')]
    pallas_call x0 -> x1, Pallas kernels: none -> 98.4 us  [per_device(): pl.pallas_call(functools.partial(kernel, nh), out_shape=jax.ShapeDtypeStr...]
    dot_general x21 -> x0, matrix products: 63.2 us -> none  [the longest x5 23.6 us: update_rows(): jnp.einsum('hij,hjk->hik', polynomial, full_iterate, preferred_element_ty...]
    all_to_all x4 -> x0, starting transfers between devices: 17.2 us -> none  [the longest x1 6.2 us: per_device(): lax.all_to_all(rates, 'head', split_axis=1, concat_axis=0, tiled=True)]
    all_to_all x4 -> x0, waiting for transfers between devices: 14.7 us -> none  [the longest x1 8.7 us: per_device(): lax.all_to_all(keys_n, 'head', split_axis=1, concat_axis=0, tiled=True)]
    all_to_all x1 -> x0, blocking collectives: 12.8 us -> none  [per_device(): lax.all_to_all(normed.reshape(token_rows, heads_here * width), 'head', sp...]
    reduce_sum x4 -> x0, other arithmetic: 6.54 us -> none  [the longest x2 4.99 us: orthogonal(): jnp.sum(gradient * gradient, axis=(1, 2), keepdims=True)]
    all_to_all x5 -> x0, local copies, waits for them, and re-layouts: 4.9 us -> none  [the longest x1 1.28 us: per_device(): lax.all_to_all(rates, 'head', split_axis=1, concat_axis=0, tiled=True)]
  transfers between devices with their start and end apart: 5 -> 0, of which waited for: 4 -> 0; matrix products, arithmetic and copies ran while one was open for 13% -> 0% of each run, Pallas kernels for 0% -> 0%
where the time goes in v1:
time: 102 us
  Pallas kernels  98.4 us (96%)
  local copies, waits for them, and re-layouts  3.34 us (3%)
    pallas_call x1, Pallas kernels, per_device(): pl.pallas_call(functools.partial(kernel, nh), out_shape=jax.ShapeDtypeStr...  98.4 us
    unnamed x2, local copies, waits for them, and re-layouts  3.34 us

profile of v1, /device:TPU:1, one launch (start us, length us, event | category | flops | bytes accessed | tf_op | source)
XLA Modules:
  0.0 101.7 jit_solution(14796360763971531038)
XLA Ops:
  0.0 1.4 %copy.10.r_ref = bf16[64,8]{1,0:T(8,128)(2,1)} copy(bf16[64,8]{0,1:T(8,128)(2,1)} %param.12) | data formatting | bytes 2048 | tf_op args[3]
  1.4 98.4 %span.1 = bf16[64,5120]{1,0:T(8,128)(2,1)} custom-call(bf16[64,5120]{1,0:T(8,128)(2,1)} %q_ref.1, bf16[64,5120]{1,0:T(8,128)(2,1)} %k_ref.1, bf16[64,5120]{1,0:T(8,128)(2,1)} %v_ref.1, bf16[64,8]{1,0:T(8,128)(2,1)} %copy.10.r_ref, f32[1,5120]{1,0:T(1,128)} %bitcast.2, f32[1,5120]{1,0:T(1,128)} %bitcast.3, f32[1,640,640]{2,1,0:T(8,128)} %w1_hbm.1, ...), custom_call_target="tpu_custom_call" | custom-call | tf_op jit(solution)/shard_map/span/pallas_call | solution.py:405
  99.8 2.0 %copy.12 = bf16[64,5120]{1,0:T(8,128)(2,1)} copy(bf16[64,5120]{1,0:T(8,128)(2,1)} %span.1) | data formatting | bytes 1310720
